TPU v7x, 32 devices: a whole 2x2x4 slice. The times are simulated.
32 devices in a mesh: dp: 2 (over x), expert: 8 (over z, y), tensor: 2 (over core).
Axes of the slice: x: 2, y: 2, z: 4, core: 2. Of those that a mesh axis runs over, the one named last changes fastest.
Arguments:
- activations: bfloat16 [4096, 1536], P(('dp', 'expert', 'tensor')), may hold values from -6 to 6
- segments: int32 [16, 256], P(('dp', 'expert')), may hold values from 0 to 3, never falling along the last dimension, each value on 1 to 128 neighbouring positions
- routes: int32 [4096, 8], P(('dp', 'expert', 'tensor')), may hold values from 0 to 15, all different within a row; in each aligned block of 128 rows (0 to 127, 128 to 255, ...) at most 128 rows name the same one
- route_weights: float32 [4096, 8], P(('dp', 'expert', 'tensor')), may hold values from 0.03 to 0.3
- norm_attn_gain: float32 [1536], replicated, may hold values from 0.5 to 1.5
- norm_ffn_gain: float32 [1536], replicated, may hold values from 0.5 to 1.5
- query_weight: bfloat16 [1536, 1536], P(None, 'tensor'), may hold values from -0.15625 to 0.15625
- key_matrix: bfloat16 [1536, 512], P(None, 'tensor'), may hold values from -0.15625 to 0.15625
- value_matrix: bfloat16 [1536, 512], P(None, 'tensor'), may hold values from -0.15625 to 0.15625
- output_projection_weight: bfloat16 [1536, 1536], P('tensor'), may hold values from -0.625 to 0.625
- expert_gate: bfloat16 [16, 1536, 512], P('expert', None, 'tensor'), may hold values from -0.15625 to 0.15625
- expert_up: bfloat16 [16, 1536, 512], P('expert', None, 'tensor'), may hold values from -0.15625 to 0.15625
- expert_down: bfloat16 [16, 512, 1536], P('expert', 'tensor'), may hold values from -0.5 to 0.5
- grad_output: bfloat16 [4096, 1536], P(('dp', 'expert', 'tensor')), may hold values from -6 to 6
Outputs:
- block_out: bfloat16 [4096, 1536], P(('dp', 'expert', 'tensor'))
- grad_input: float32 [4096, 1536], P(('dp', 'expert', 'tensor'))
- grad_norm_attn: float32 [1536], replicated
- grad_norm_ffn: float32 [1536], replicated
- grad_query: float32 [1536, 1536], P(None, 'tensor')
- grad_key: float32 [1536, 512], P(None, 'tensor')
- grad_value: float32 [1536, 512], P(None, 'tensor')
- grad_mixer: float32 [1536, 1536], P('tensor')
- grad_expert_gate: float32 [16, 1536, 512], P('expert', None, 'tensor')
- grad_expert_up: float32 [16, 1536, 512], P('expert', None, 'tensor')
- grad_expert_down: float32 [16, 512, 1536], P('expert', 'tensor')
Inputs may be any that keep to these rules, and one draw needn't show every extreme that they name: `routes`: each row names 8 different experts; in the rows of one device (aligned blocks of 128 rows) no expert is named more than 128 times, and one is named exactly 128 times in some block. `segments`: each sequence's numbers never fall; 4 documents of 1 to 128 positions, one of exactly 128.
All inputs are finite; a program needn't handle non-finite values.
Results may differ from a plain program's by a relative error of at most 0.01.
Values may be sent and summed in bfloat16 or wider, within the bound.
No kernel may reach another device: no remote copies, remote signals or barrier semaphores. Data moves between devices by JAX's collectives and lax.ppermute only.
A program may use at most 320 MiB of HBM per device.

v0:
```python
import jax
import jax.numpy as jnp
from jax import lax
from jax.sharding import PartitionSpec as P

HEAD_DIM = 64
EPS = 1e-05
ATTN_SCALE = 0.015625
THETA = 10000.0
NEG_FILL = -1e30


def norm_forward(values, gain_vector):
    inv_scale = lax.rsqrt(jnp.mean(values * values, axis=-1, keepdims=True) + EPS)
    return (values * inv_scale * gain_vector, inv_scale)


def norm_backward(values, inv_scale, gain_vector, upstream):
    weighted = upstream * gain_vector
    inner = jnp.mean(weighted * values, axis=-1, keepdims=True)
    value_gradient = inv_scale * weighted - values * (inv_scale * inv_scale * inv_scale) * inner
    grad_gain = jnp.sum(upstream * values * inv_scale, axis=0)
    return (value_gradient, grad_gain)


def rope_tables(length, head_size):
    position = jnp.arange(length, dtype=jnp.float32)
    frequency = THETA ** (-jnp.arange(head_size // 2, dtype=jnp.float32) * 2.0 / head_size)
    angle_table = position[:, None] * frequency[None, :]
    return (jnp.cos(angle_table)[:, None, :], jnp.sin(angle_table)[:, None, :])


def apply_rotary(field_in, cosine_lookup, sine_lookup):
    half_size = field_in.shape[-1] // 2
    first_half = field_in[..., :half_size]
    second_half = field_in[..., half_size:]
    return jnp.concatenate(
        [
            first_half * cosine_lookup - second_half * sine_lookup,
            second_half * cosine_lookup + first_half * sine_lookup,
        ],
        axis=-1,
    )


def invert_rotary(field_in, cosine_lookup, sine_lookup):
    half_size = field_in.shape[-1] // 2
    first_half = field_in[..., :half_size]
    second_half = field_in[..., half_size:]
    return jnp.concatenate(
        [
            first_half * cosine_lookup + second_half * sine_lookup,
            second_half * cosine_lookup - first_half * sine_lookup,
        ],
        axis=-1,
    )


def mask_block(row_start, block_rows, seg_ids):
    length = seg_ids.shape[0]
    row_pos = row_start + jnp.arange(block_rows, dtype=jnp.int32)
    key_pos = jnp.arange(length, dtype=jnp.int32)
    return (key_pos[None, :] <= row_pos[:, None]) & (seg_ids[None, :] == seg_ids[:, None])


def block_scores(query_blk, key_heads, row_start, seg_ids):
    scores = (
        jnp.einsum("qhgd,khd->hgqk", query_blk, key_heads, preferred_element_type=jnp.float32)
        * ATTN_SCALE
    )
    allowed = mask_block(row_start, query_blk.shape[0], seg_ids)
    return jnp.where(allowed, scores, NEG_FILL)


def attend_block(query_blk, key_heads, value_head_rows, row_start, seg_ids):
    scores = block_scores(query_blk, key_heads, row_start, seg_ids)
    top_score = jnp.max(scores, axis=-1, keepdims=True)
    exp_total = jnp.sum(jnp.exp(scores - top_score), axis=-1, keepdims=True)
    log_total = top_score + jnp.log(exp_total)
    weights_soft = jnp.exp(scores - log_total).astype(jnp.bfloat16)
    mixed_heads = jnp.einsum(
        "hgqk,khd->qhgd", weights_soft, value_head_rows, preferred_element_type=jnp.float32
    )
    return (mixed_heads.astype(jnp.bfloat16), log_total[..., 0])


def attend_back(
    query_blk, key_heads, value_head_rows, log_total, grad_blk, mixed_blk, row_start, seg_ids
):
    scores = block_scores(query_blk, key_heads, row_start, seg_ids)
    weights_soft = jnp.exp(scores - log_total[..., None])
    row_delta = jnp.einsum(
        "qhgd,qhgd->hgq", grad_blk, mixed_blk, preferred_element_type=jnp.float32
    )
    grad_soft = jnp.einsum(
        "qhgd,khd->hgqk", grad_blk, value_head_rows, preferred_element_type=jnp.float32
    )
    grad_scores = (weights_soft * (grad_soft - row_delta[..., None]) * ATTN_SCALE).astype(
        jnp.bfloat16
    )
    grad_queries = jnp.einsum(
        "hgqk,khd->qhgd", grad_scores, key_heads, preferred_element_type=jnp.float32
    )
    key_gradient = jnp.einsum(
        "hgqk,qhgd->khd", grad_scores, query_blk, preferred_element_type=jnp.float32
    )
    value_gradient = jnp.einsum(
        "hgqk,qhgd->khd",
        weights_soft.astype(jnp.bfloat16),
        grad_blk,
        preferred_element_type=jnp.float32,
    )
    return (grad_queries, key_gradient, value_gradient)


def route_index(route_blk, expert_count, capacity):
    flat_routes = route_blk.reshape(-1)
    onehot = (flat_routes[:, None] == jnp.arange(expert_count, dtype=jnp.int32)[None, :]).astype(
        jnp.int32
    )
    earlier = jnp.cumsum(onehot, axis=0) - onehot
    slot_rank = jnp.sum(earlier * onehot, axis=1)
    return flat_routes * capacity + slot_rank


def body(
    activations,
    segments,
    routes,
    route_weights,
    norm_attn_gain,
    norm_ffn_gain,
    query_weight,
    key_matrix,
    value_matrix,
    output_projection_weight,
    expert_gate,
    expert_up,
    expert_down,
    grad_output,
):
    tensor_rank = lax.axis_index("tensor")
    tok_rows = activations.shape[0]
    model_width = activations.shape[1]
    experts_here = expert_gate.shape[0]
    expert_count = experts_here * lax.axis_size("expert")
    top_count = routes.shape[1]
    capacity = 2 * tok_rows * top_count // expert_count
    seg_ids = segments[0]
    length = seg_ids.shape[0]
    heads_q = query_weight.shape[1] // HEAD_DIM
    heads_kv = key_matrix.shape[1] // HEAD_DIM
    group_factor = heads_q // heads_kv
    block_rows = min(512, length)
    blocks = length // block_rows
    cosine_lookup, sine_lookup = rope_tables(length, HEAD_DIM)
    own_start = tensor_rank * tok_rows
    full_acts = lax.all_gather(activations, "tensor", axis=0, tiled=True)
    x_in = full_acts.astype(jnp.float32)
    normed_one, scale_one = norm_forward(x_in, norm_attn_gain)
    hidden_first = normed_one.astype(jnp.bfloat16)
    query_unrotated = jnp.dot(
        hidden_first, query_weight, preferred_element_type=jnp.float32
    ).reshape(length, heads_q, HEAD_DIM)
    query_head_rows = (
        apply_rotary(query_unrotated, cosine_lookup, sine_lookup)
        .astype(jnp.bfloat16)
        .reshape(length, heads_kv, group_factor, HEAD_DIM)
    )
    key_unrotated = jnp.dot(hidden_first, key_matrix, preferred_element_type=jnp.float32).reshape(
        length, heads_kv, HEAD_DIM
    )
    key_heads = apply_rotary(key_unrotated, cosine_lookup, sine_lookup).astype(jnp.bfloat16)
    value_head_rows = (
        jnp.dot(hidden_first, value_matrix, preferred_element_type=jnp.float32)
        .astype(jnp.bfloat16)
        .reshape(length, heads_kv, HEAD_DIM)
    )
    query_blocks = query_head_rows.reshape(blocks, block_rows, heads_kv, group_factor, HEAD_DIM)
    starts = jnp.arange(blocks, dtype=jnp.int32) * block_rows

    def forward_block(block_pair):
        return attend_block(block_pair[0], key_heads, value_head_rows, block_pair[1], seg_ids)

    mixed_heads, log_total = lax.map(forward_block, (query_blocks, starts))
    mixed_flat = mixed_heads.reshape(length, heads_q * HEAD_DIM)
    attn_part = jnp.dot(mixed_flat, output_projection_weight, preferred_element_type=jnp.float32)
    attn_out = lax.psum(attn_part, "tensor")
    residual = x_in + attn_out
    normed_two, scale_two = norm_forward(residual, norm_ffn_gain)
    h_two = normed_two.astype(jnp.bfloat16)
    h_own = lax.dynamic_slice_in_dim(h_two, own_start, tok_rows, 0)
    resid_own = lax.dynamic_slice_in_dim(residual, own_start, tok_rows, 0)
    slot_index = route_index(routes, expert_count, capacity)
    buffer = (
        jnp.zeros((expert_count * capacity, model_width), jnp.bfloat16)
        .at[slot_index]
        .set(jnp.repeat(h_own, top_count, axis=0))
        .reshape(expert_count, capacity, model_width)
    )
    received = lax.all_to_all(buffer, "expert", split_axis=0, concat_axis=1, tiled=True)
    gate_full, up_full, down_full = (expert_gate, expert_up, expert_down)
    rows_in = lax.all_gather(received, "tensor", axis=1, tiled=True)
    pre_gate = jnp.einsum("erd,edf->erf", rows_in, gate_full, preferred_element_type=jnp.float32)
    pre_up = jnp.einsum("erd,edf->erf", rows_in, up_full, preferred_element_type=jnp.float32)
    activated = (jax.nn.silu(pre_gate) * pre_up).astype(jnp.bfloat16)
    expert_part = jnp.einsum(
        "erf,efd->erd", activated, down_full, preferred_element_type=jnp.float32
    )
    expert_total = lax.psum_scatter(
        expert_part.astype(jnp.bfloat16), "tensor", scatter_dimension=1, tiled=True
    )
    returned = lax.all_to_all(expert_total, "expert", split_axis=1, concat_axis=0, tiled=True)
    picked = returned.reshape(-1, model_width)[slot_index].reshape(tok_rows, top_count, model_width)
    expert_mix = jnp.sum(route_weights[:, :, None] * picked.astype(jnp.float32), axis=1)
    block_out = (resid_own + expert_mix).astype(jnp.bfloat16)
    upstream_own = grad_output.astype(jnp.float32)
    grad_copies = (
        (route_weights[:, :, None] * upstream_own[:, None, :])
        .astype(jnp.bfloat16)
        .reshape(-1, model_width)
    )
    grad_buffer = (
        jnp.zeros((expert_count * capacity, model_width), jnp.bfloat16)
        .at[slot_index]
        .set(grad_copies)
        .reshape(expert_count, capacity, model_width)
    )
    grad_received = lax.all_to_all(grad_buffer, "expert", split_axis=0, concat_axis=1, tiled=True)
    grad_rows_in = lax.all_gather(grad_received, "tensor", axis=1, tiled=True)
    grad_down = jnp.einsum(
        "erf,erd->efd", activated, grad_rows_in, preferred_element_type=jnp.float32
    )
    grad_act = jnp.einsum(
        "erd,efd->erf", grad_rows_in, down_full, preferred_element_type=jnp.float32
    )
    gate_sigmoid = jax.nn.sigmoid(pre_gate)
    grad_pre_gate = (
        grad_act * pre_up * gate_sigmoid * (1.0 + pre_gate * (1.0 - gate_sigmoid))
    ).astype(jnp.bfloat16)
    grad_pre_up = (grad_act * pre_gate * gate_sigmoid).astype(jnp.bfloat16)
    grad_gate = jnp.einsum(
        "erd,erf->edf", rows_in, grad_pre_gate, preferred_element_type=jnp.float32
    )
    grad_up = jnp.einsum("erd,erf->edf", rows_in, grad_pre_up, preferred_element_type=jnp.float32)
    grad_in_part = jnp.einsum(
        "erf,edf->erd", grad_pre_gate, gate_full, preferred_element_type=jnp.float32
    ) + jnp.einsum("erf,edf->erd", grad_pre_up, up_full, preferred_element_type=jnp.float32)
    grad_in_rows = lax.psum_scatter(grad_in_part, "tensor", scatter_dimension=1, tiled=True)
    grad_back = lax.all_to_all(
        grad_in_rows.astype(jnp.bfloat16), "expert", split_axis=1, concat_axis=0, tiled=True
    )
    picked_grad = grad_back.reshape(-1, model_width)[slot_index].reshape(
        tok_rows, top_count, model_width
    )
    grad_h_own = jnp.sum(route_weights[:, :, None] * picked_grad.astype(jnp.float32), axis=1)
    upstream_full, grad_h_full = (
        lax.all_gather(upstream_own, "tensor", axis=0, tiled=True),
        lax.all_gather(grad_h_own, "tensor", axis=0, tiled=True),
    )
    grad_norm_part, grad_ffn_gain = norm_backward(residual, scale_two, norm_ffn_gain, grad_h_full)
    grad_resid = upstream_full + grad_norm_part
    residual_gradient_second = grad_resid.astype(jnp.bfloat16)
    grad_mix_w = jnp.einsum(
        "sa,sb->ab", mixed_flat, residual_gradient_second, preferred_element_type=jnp.float32
    )
    mixed_gradient = (
        jnp.einsum(
            "im,dm->id",
            residual_gradient_second,
            output_projection_weight,
            preferred_element_type=jnp.float32,
        )
        .astype(jnp.bfloat16)
        .reshape(blocks, block_rows, heads_kv, group_factor, HEAD_DIM)
    )

    def backward_block(block_pack):
        return attend_back(
            block_pack[0],
            key_heads,
            value_head_rows,
            block_pack[1],
            block_pack[2],
            block_pack[3],
            block_pack[4],
            seg_ids,
        )

    grad_queries, key_gradient, value_gradient = lax.map(
        backward_block, (query_blocks, log_total, mixed_gradient, mixed_heads, starts)
    )
    key_gradient = jnp.sum(key_gradient, axis=0)
    value_gradient = jnp.sum(value_gradient, axis=0)
    grad_q_rows = (
        invert_rotary(grad_queries.reshape(length, heads_q, HEAD_DIM), cosine_lookup, sine_lookup)
        .astype(jnp.bfloat16)
        .reshape(length, heads_q * HEAD_DIM)
    )
    grad_key_rows = (
        invert_rotary(key_gradient, cosine_lookup, sine_lookup)
        .astype(jnp.bfloat16)
        .reshape(length, heads_kv * HEAD_DIM)
    )
    grad_value_rows = value_gradient.astype(jnp.bfloat16).reshape(length, heads_kv * HEAD_DIM)
    grad_q_w = jnp.einsum(
        "sd,sa->da", hidden_first, grad_q_rows, preferred_element_type=jnp.float32
    )
    grad_k_w = jnp.einsum(
        "sd,sa->da", hidden_first, grad_key_rows, preferred_element_type=jnp.float32
    )
    grad_v_w = jnp.einsum(
        "sd,sa->da", hidden_first, grad_value_rows, preferred_element_type=jnp.float32
    )
    grad_h_part = (
        jnp.einsum("sa,da->sd", grad_q_rows, query_weight, preferred_element_type=jnp.float32)
        + jnp.einsum("sa,da->sd", grad_key_rows, key_matrix, preferred_element_type=jnp.float32)
        + jnp.einsum("sa,da->sd", grad_value_rows, value_matrix, preferred_element_type=jnp.float32)
    )
    grad_h_one = lax.psum(grad_h_part, "tensor")
    grad_x_part, grad_attn_gain = norm_backward(x_in, scale_one, norm_attn_gain, grad_h_one)
    grad_full = grad_resid + grad_x_part
    grad_input = lax.dynamic_slice_in_dim(grad_full, own_start, tok_rows, 0)
    dense_sums = lax.psum(
        (grad_attn_gain, grad_ffn_gain, grad_q_w, grad_k_w, grad_v_w, grad_mix_w), ("dp", "expert")
    )
    gate_half, up_half, down_half = (grad_gate, grad_up, grad_down)
    gate_sum, up_sum, down_sum = lax.psum((gate_half, up_half, down_half), "dp")
    return (
        block_out,
        grad_input,
        dense_sums[0],
        dense_sums[1],
        dense_sums[2],
        dense_sums[3],
        dense_sums[4],
        dense_sums[5],
        gate_sum,
        up_sum,
        down_sum,
    )


def solution(mesh):
    placed = (
        P(("dp", "expert", "tensor"), None),
        P(("dp", "expert"), None),
        P(("dp", "expert", "tensor"), None),
        P(("dp", "expert", "tensor"), None),
        P(),
        P(),
        P(None, "tensor"),
        P(None, "tensor"),
        P(None, "tensor"),
        P("tensor", None),
        P("expert", None, "tensor"),
        P("expert", None, "tensor"),
        P("expert", "tensor", None),
        P(("dp", "expert", "tensor"), None),
    )
    return jax.shard_map(
        body,
        mesh=mesh,
        in_specs=placed,
        out_specs=(
            P(("dp", "expert", "tensor"), None),
            P(("dp", "expert", "tensor"), None),
            P(),
            P(),
            P(None, "tensor"),
            P(None, "tensor"),
            P(None, "tensor"),
            P("tensor", None),
            P("expert", None, "tensor"),
            P("expert", None, "tensor"),
            P("expert", "tensor", None),
        ),
        check_vma=False,
    )
```

profile of v0, /device:TPU:0, one launch (start us, length us, event | category | flops | bytes accessed | tf_op | source)
XLA Modules:
  0.0 1433.3 jit_solution(16432259173664442176)
XLA Ops:
  9.0 4.5 reduce-window.6
  16.2 9.6 scatter_custom_fusion.1
  25.8 7.4 all-to-all-start.2
  33.3 3.2 all_gather.15
  37.7 1.7 fusion.56
  46.1 1.9 fusion.59
  48.1 123.4 %all-to-all-done.2 = bf16[16,128,1536]{2,1,0:T(8,128)(2,1)} async-done(((bf16[16,128,1536]{2,1,0:T(8,128)(2,1)}), bf16[16,128,1536]{2,1,0:T(8,128)(2,1)}, u32[]{:S(2)}, u32[]{:S(2)}) %all-to-all-start.2) | async-done | bytes 6291488 | tf_op jit(solution)/shard_map/all_to_all | solution.py:229
  171.5 6.0 copy.77
  180.6 9.9 scatter_custom_fusion
  190.5 142.7 %all_to_all.66 = bf16[16,128,1536]{2,1,0:T(8,128)(2,1)S(1)} all-to-all(bf16[16,128,1536]{2,1,0:T(8,128)(2,1)} %bitcast.164), channel_id=1, replica_groups=mesh['dp'=2,'expert'=8,'tensor'=2] {'expert'}, dimensions={0} | all-to-all | bytes 12582912 | tf_op jit(solution)/shard_map/all_to_all | solution.py:201
  333.2 3.3 copy.73
  336.6 11.0 fusion.61
  347.6 12.6 all-gather.5.cloned.1.call-done
  360.2 7.0 fusion.60
  367.2 9.4 multiply_convert_fusion.2
  378.0 6.4 convolution_convert_fusion
  384.6 19.7 %fusion.62 = f32[2,2048,1536]{2,1,0:T(8,128)} fusion(bf16[2,2048,256]{2,1,0:T(8,128)(2,1)} %get-tuple-element.84, bf16[2,1536,256]{2,1,0:T(8,128)(2,1)} %param.24), kind=kOutput, calls=%fused_computation.122 | convolution fusion | flops 3221225472 | bytes 28835840 | tf_op jit(solution)/shard_map/erf,edf->erd/dot_general | solution.py:246
  404.3 21.5 %convolution_add_fusion = f32[2,2048,1536]{2,1,0:T(8,128)} fusion(f32[2,2048,1536]{2,1,0:T(8,128)} %fusion.62, bf16[2,2048,256]{2,1,0:T(8,128)(2,1)} %get-tuple-element.85, bf16[2,1536,256]{2,1,0:T(8,128)(2,1)} %param.25), kind=kOutput, calls=%fused_computation.4 | convolution fusion | flops 3227516928 | bytes 54001664 | tf_op jit(solution)/shard_map/erf,edf->erd/dot_general | solution.py:248
  425.8 12.8 copy.74
  438.7 5.8 all-to-all-start.1
  444.5 18.1 %reduce-scatter.5.cloned.1.call-done = f32[2,1024,1536]{2,1,0:T(8,128)} async-done(((f32[2,2048,1536]{2,1,0:T(8,128)}), f32[2,1024,1536]{2,1,0:T(8,128)}) %reduce-scatter.5.cloned.1.call-update) | async-done | bytes 12582928 | tf_op jit(solution)/shard_map/reduce_scatter | solution.py:249
  462.6 8.0 convert_element_type.120
  470.6 12.7 copy.78
  483.4 99.8 %all-to-all-done.1 = bf16[2,1024,1536]{2,0,1:T(2,128)(2,1)} async-done(((bf16[2,1024,1536]{2,0,1:T(2,128)(2,1)}), bf16[2,1024,1536]{2,0,1:T(2,128)(2,1)}, u32[]{:S(2)}, u32[]{:S(2)}) %all-to-all-start.1) | async-done | bytes 6291488 | tf_op jit(solution)/shard_map/all_to_all | solution.py:213
  583.1 4.7 all-to-all-start.3
  588.4 6.7 copy.75
  595.1 10.9 gather_fusion
  606.0 119.7 %all-to-all-done.3 = bf16[2,1024,1536]{2,0,1:T(2,128)(2,1)} async-done(((bf16[2,1024,1536]{2,0,1:T(2,128)(2,1)}), bf16[2,1024,1536]{2,0,1:T(2,128)(2,1)}, u32[]{:S(2)}, u32[]{:S(2)}) %all-to-all-start.3) | async-done | bytes 6291488 | tf_op jit(solution)/shard_map/all_to_all | solution.py:250
  725.6 6.7 copy.79
  732.3 10.9 gather_fusion.1
  743.1 8.7 fusion
  752.9 12.1 fusion.64
  765.0 2.9 multiply_reduce_fusion
  767.9 6.2 all-gather.7.cloned.1.call-done
  774.1 2.8 subtract_add_fusion
  779.0 2.9 fusion.23
  789.8 11.8 fusion.65
  801.7 10.4 fusion.66
  813.2 2.6 fusion.48
  817.5 3.1 fusion.52
  820.7 3.0 fusion.27
  826.7 2.9 fusion.21
  829.7 78.3 %all-reduce = (f32[1536]{0:T(1024)}, f32[1536]{0:T(1024)}) all-reduce(f32[1536]{0:T(1024)S(1)} %get-tuple-element.56, f32[1536]{0:T(1024)S(1)} %copy-done.51), channel_id=1, replica_groups=mesh['dp'=2,'expert'=8,'tensor'=2] {'dp','expert'}, use_global_device_ids=true, to_apply=%region_18.19 | all-reduce | flops 3072 | bytes 24576 | tf_op jit(solution)/shard_map/psum | solution.py:324
  908.0 2.7 dynamic-slice_add_fusion
  910.8 127.0 %all-reduce.14.cloned.1.call-done = (f32[2,1536,256]{2,1,0:T(8,128)}, f32[2,1536,256]{2,1,0:T(8,128)}, f32[2,256,1536]{2,1,0:T(8,128)}) async-done(((f32[2,1536,256]{2,1,0:T(8,128)}, f32[2,1536,256]{2,1,0:T(8,128)}, f32[2,256,1536]{2,1,0:T(8,128)}), (f32[2,1536,256]{2,1,0:T(8,128)}, f32[2,1536,256]{2,1,0:T(8,128)}, f32[2,256,1536]{2,1,0:T(8,128)})) %all-reduce.14.cloned.1.call-update) | async-done | bytes 9437200 | tf_op jit(solution)/shard_map/psum | solution.py:328
  1037.7 368.7 %all-reduce.12.cloned.1.call-done = (f32[1536,768]{1,0:T(8,128)}, f32[1536,256]{1,0:T(8,128)}, f32[1536,256]{1,0:T(8,128)}, f32[768,1536]{1,0:T(8,128)}) async-done(((f32[1536,768]{1,0:T(8,128)}, f32[1536,256]{1,0:T(8,128)}, f32[1536,256]{1,0:T(8,128)}, f32[768,1536]{1,0:T(8,128)}), (f32[1536,768]{1,0:T(8,128)}, f32[1536,256]{1,0:T(8,128)}, f32[1536,256]{1,0:T(8,128)}, ...) | async-done | bytes 12582928 | tf_op jit(solution)/shard_map/psum | solution.py:324
  1406.4 5.0 copy.119
  1414.9 2.4 copy.122
  (205 shorter events, 46.5 us)
Async XLA Ops:
  7.2 38.9 %copy-start = (bf16[768,1536]{1,0:T(8,128)(2,1)S(1)}, bf16[768,1536]{1,0:T(8,128)(2,1)}, u32[]{:S(2)}) copy-start(bf16[768,1536]{1,0:T(8,128)(2,1)} %param.23) | copy-start | bytes 7077892
  15.2 10.6 copy-start.8
  25.8 11.7 copy-start.54
  25.8 11.8 copy-start.40
  25.8 145.6 %all-to-all-start.2 = ((bf16[16,128,1536]{2,1,0:T(8,128)(2,1)}), bf16[16,128,1536]{2,1,0:T(8,128)(2,1)}, u32[]{:S(2)}, u32[]{:S(2)}) async-start(bf16[16,128,1536]{2,1,0:T(8,128)(2,1)} %bitcast.162), calls=%async_computation.3 | async-start | bytes 12582912 | tf_op jit(solution)/shard_map/all_to_all | solution.py:229
  33.3 144.3 %all-reduce.8.cloned.1.call-start = ((), (), s32[]{:S(2)}) async-start(), calls=%async_computation.6 | async-start | bytes 3145728 | tf_op jit(solution)/shard_map/psum | solution.py:188
  33.3 6.1 copy-start.20
  36.5 141.1 %copy-start.1 = (bf16[256,1536]{1,0:T(8,128)(2,1)}, bf16[256,1536]{1,0:T(8,128)(2,1)S(1)}, u32[]{:S(2)}) copy-start(bf16[256,1536]{1,0:T(8,128)(2,1)S(1)} %all_gather.15) | copy-start | bytes 2359300
  37.3 5.5 copy-start.49
  37.5 3.1 copy-start.28
  37.5 3.1 copy-start.30
  37.7 6.8 copy-start.46
  42.1 2.3 copy-start.14
  42.2 1.7 copy-start.37
  48.0 288.6 %all-gather.9.cloned.1.call-start = ((), (), s32[]{:S(2)}) async-start(), calls=%async_computation.10 | async-start | bytes 18874368 | tf_op jit(solution)/shard_map/all_gather | solution.py:230
  177.5 2.9 copy-start.48
  177.5 182.6 %all-gather.5.cloned.1.call-start = ((), (), s32[]{:S(2)}) async-start(), calls=%async_computation.7 | async-start | bytes 18874368 | tf_op jit(solution)/shard_map/all_gather | solution.py:203
  336.5 89.3 %reduce-scatter.3.cloned.1.call-start = ((), (), s32[]{:S(2)}) async-start(), calls=%async_computation.8 | async-start | bytes 18874368 | tf_op jit(solution)/shard_map/reduce_scatter | solution.py:210
  360.2 7.0 copy-start.22
  360.2 7.0 copy-start.58
  367.2 10.8 copy-start.25
  384.3 78.2 %reduce-scatter.5.cloned.1.call-start = ((), (), s32[]{:S(2)}) async-start(), calls=%async_computation.11 | async-start | bytes 37748736 | tf_op jit(solution)/shard_map/reduce_scatter | solution.py:249
  438.7 144.5 %all-to-all-start.1 = ((bf16[2,1024,1536]{2,0,1:T(2,128)(2,1)}), bf16[2,1024,1536]{2,0,1:T(2,128)(2,1)}, u32[]{:S(2)}, u32[]{:S(2)}) async-start(bf16[2,1024,1536]{2,0,1:T(2,128)(2,1)} %copy.74), calls=%async_computation.2 | async-start | bytes 12582912 | tf_op jit(solution)/shard_map/all_to_all | solution.py:213
  583.1 142.5 %all-to-all-start.3 = ((bf16[2,1024,1536]{2,0,1:T(2,128)(2,1)}), bf16[2,1024,1536]{2,0,1:T(2,128)(2,1)}, u32[]{:S(2)}, u32[]{:S(2)}) async-start(bf16[2,1024,1536]{2,0,1:T(2,128)(2,1)} %copy.78), calls=%async_computation.5 | async-start | bytes 12582912 | tf_op jit(solution)/shard_map/all_to_all | solution.py:250
  587.9 177.1 %all-gather.11.cloned.1.call-start = ((), (), s32[]{:S(2)}) async-start(), calls=%async_computation.12 | async-start | bytes 2359296 | tf_op jit(solution)/shard_map/all_gather | solution.py:259
  751.9 22.2 %all-gather.7.cloned.1.call-start = ((), (), s32[]{:S(2)}) async-start(), calls=%async_computation.9 | async-start | bytes 2359296 | tf_op jit(solution)/shard_map/all_gather | solution.py:258
  752.6 74.0 %all-reduce.10.cloned.1.call-start = ((), (), s32[]{:S(2)}) async-start(), calls=%async_computation.13 | async-start | bytes 3145728 | tf_op jit(solution)/shard_map/psum | solution.py:320
  779.0 2.9 copy-start.10
  779.0 3.0 copy-start.15
  779.0 3.0 copy-start.47
  779.0 3.0 copy-start.57
  781.9 5.4 copy-start.39
  785.1 2.2 copy-start.12
  785.1 1.7 copy-start.36
  789.6 248.1 %all-reduce.14.cloned.1.call-start = ((), (), s32[]{:S(2)}) async-start(), calls=%async_computation.15 | async-start | bytes 18874368 | tf_op jit(solution)/shard_map/psum | solution.py:328
  812.1 594.3 %all-reduce.12.cloned.1.call-start = ((), (), s32[]{:S(2)}) async-start(), calls=%async_computation.14 | async-start | bytes 25165824 | tf_op jit(solution)/shard_map/psum | solution.py:324
  813.2 2.6 copy-start.27
  813.2 4.3 copy-start.13
  817.5 3.1 copy-start.7
  823.7 1.9 copy-start.5
  823.7 2.2 copy-start.19
  826.7 3.0 copy-start.51
  1406.4 5.0 copy-start.24
  1406.4 6.1 copy-start.23
  1411.4 3.5 copy-start.11
  1414.9 3.6 copy-start.18
  1418.5 3.0 copy-start.17
  1421.5 3.0 copy-start.16
  (24 other events, 28.4 us)
Sparse Core Ops, SparseCore 0:
  48.2 21.7 all-reduce.7
  177.6 23.4 all-gather.8
  336.6 23.4 all-gather.4
  384.4 22.6 reduce-scatter.2
  425.9 36.6 reduce-scatter.4
  752.0 8.8 all-gather.10
  763.0 10.9 all-gather.6
  789.7 21.5 all-reduce.9
  814.5 223.1 all-reduce.13
  1044.6 361.8 all-reduce.11
where the time goes:
time: 1440 us; the launch traced here: 1430 us
  waiting for transfers between devices  876 us (61%)
  blocking collectives  224 us (16%)
  matrix products  135 us (9%)
  local copies, waits for them, and re-layouts  112 us (8%)
  other arithmetic  50.5 us (4%)
  starting transfers between devices  19.3 us (1%)
  between operations  15.2 us (1%)
    psum x1, waiting for transfers between devices, body(): lax.psum((grad_attn_gain, grad_ffn_gain, grad_q_w, grad_k_w, grad_v_w, gr...  369 us
    all_to_all x1, blocking collectives, body(): lax.all_to_all(buffer, 'expert', split_axis=0, concat_axis=1, tiled=True)  143 us
    psum x1, waiting for transfers between devices, body(): gate_sum, up_sum, down_sum = lax.psum((gate_half, up_half, down_half), 'dp')  127 us
    all_to_all x1, waiting for transfers between devices, body(): lax.all_to_all(grad_buffer, 'expert', split_axis=0, concat_axis=1, tiled=...  123 us
    all_to_all x1, waiting for transfers between devices, body(): lax.all_to_all(grad_in_rows.astype(jnp.bfloat16), 'expert', split_axis=1,...  120 us
    all_to_all x1, waiting for transfers between devices, body(): lax.all_to_all(expert_total, 'expert', split_axis=1, concat_axis=0, tiled...  99.8 us
    psum x1, blocking collectives, body(): lax.psum((grad_attn_gain, grad_ffn_gain, grad_q_w, grad_k_w, grad_v_w, gr...  78.3 us
    unnamed x127, local copies, waits for them, and re-layouts  31.3 us
  transfers between devices with their start and end apart: 13, of which 8 were waited for; matrix products, arithmetic and copies ran while one was open for 13% of the time, Pallas kernels for 0%

commit v1 on v0

--- a/solution.py
+++ b/solution.py
@@ -322,7 +322,10 @@
     grad_full = grad_resid + grad_x_part
     grad_input = lax.dynamic_slice_in_dim(grad_full, own_start, tok_rows, 0)
     dense_sums = lax.psum(
-        (grad_attn_gain, grad_ffn_gain, grad_q_w, grad_k_w, grad_v_w, grad_mix_w), ("dp", "expert")
+        lax.psum(
+            (grad_attn_gain, grad_ffn_gain, grad_q_w, grad_k_w, grad_v_w, grad_mix_w), "expert"
+        ),
+        "dp",
     )
     gate_half, up_half, down_half = (grad_gate, grad_up, grad_down)
     gate_sum, up_sum, down_sum = lax.psum((gate_half, up_half, down_half), "dp")

time: 1440 us -> 1760 us (1.22)
  waiting for transfers between devices: 876 us -> 1220 us
  blocking collectives: 224 us -> 191 us
    psum x1, waiting for transfers between devices: 127 us -> 450 us  [body(): lax.psum(lax.psum((grad_attn_gain, grad_ffn_gain, grad_q_w, grad_k_w, gra...]
    psum x1, blocking collectives: 78.3 us -> 37.3 us  [body(): lax.psum((grad_attn_gain, grad_ffn_gain, grad_q_w, grad_k_w, grad_v_w, gr...]
    psum x1, waiting for transfers between devices: 0.01 us -> 18.7 us  [body(): grad_h_one = lax.psum(grad_h_part, 'tensor')]
  transfers between devices with their start and end apart: 13 -> 13, of which waited for: 8 -> 10; matrix products, arithmetic and copies ran while one was open for 13% -> 11% of each run, Pallas kernels for 0% -> 0%
where the time goes in v1:
time: 1760 us; the launch traced here: 1750 us
  waiting for transfers between devices  1220 us (69%)
  blocking collectives  191 us (11%)
  matrix products  135 us (8%)
  local copies, waits for them, and re-layouts  112 us (6%)
  other arithmetic  54.2 us (3%)
  starting transfers between devices  19.3 us (1%)
    psum x1, waiting for transfers between devices, body(): lax.psum(lax.psum((grad_attn_gain, grad_ffn_gain, grad_q_w, grad_k_w, gra...  450 us
    psum x1, waiting for transfers between devices, body(): lax.psum((grad_attn_gain, grad_ffn_gain, grad_q_w, grad_k_w, grad_v_w, gr...  363 us
    all_to_all x1, blocking collectives, body(): lax.all_to_all(buffer, 'expert', split_axis=0, concat_axis=1, tiled=True)  142 us
    all_to_all x1, waiting for transfers between devices, body(): lax.all_to_all(grad_buffer, 'expert', split_axis=0, concat_axis=1, tiled=...  124 us
    all_to_all x1, waiting for transfers between devices, body(): lax.all_to_all(grad_in_rows.astype(jnp.bfloat16), 'expert', split_axis=1,...  120 us
    all_to_all x1, waiting for transfers between devices, body(): lax.all_to_all(expert_total, 'expert', split_axis=1, concat_axis=0, tiled...  99.7 us
    psum x1, blocking collectives, body(): lax.psum((grad_attn_gain, grad_ffn_gain, grad_q_w, grad_k_w, grad_v_w, gr...  37.3 us
  transfers between devices with their start and end apart: 13, of which 10 were waited for; matrix products, arithmetic and copies ran while one was open for 11% of the time, Pallas kernels for 0%

profile of v1, /device:TPU:0, one launch (start us, length us, event | category | flops | bytes accessed | tf_op | source)
XLA Modules:
  0.0 1751.0 jit_solution(180023876507142427)
XLA Ops:
  10.1 4.5 reduce-window.6
  16.2 9.6 scatter_custom_fusion.1
  25.8 7.4 all-to-all-start.2
  33.3 3.0 all_gather.15
  47.9 123.6 %all-to-all-done.2 = bf16[16,128,1536]{2,1,0:T(8,128)(2,1)} async-done(((bf16[16,128,1536]{2,1,0:T(8,128)(2,1)}), bf16[16,128,1536]{2,1,0:T(8,128)(2,1)}, u32[]{:S(2)}, u32[]{:S(2)}) %all-to-all-start.2) | async-done | bytes 6291488 | tf_op jit(solution)/shard_map/all_to_all | solution.py:229
  171.4 6.0 copy.77
  181.3 10.3 scatter_custom_fusion
  191.5 142.2 %all_to_all.66 = bf16[16,128,1536]{2,1,0:T(8,128)(2,1)S(1)} all-to-all(bf16[16,128,1536]{2,1,0:T(8,128)(2,1)} %bitcast.166), channel_id=1, replica_groups=mesh['dp'=2,'expert'=8,'tensor'=2] {'expert'}, dimensions={0} | all-to-all | bytes 12582912 | tf_op jit(solution)/shard_map/all_to_all | solution.py:201
  333.7 3.3 copy.73
  337.1 11.0 fusion.61
  348.1 12.5 all-gather.5.cloned.1.call-done
  360.6 7.0 fusion.60
  367.6 9.4 multiply_convert_fusion.2
  378.4 6.3 convolution_convert_fusion
  385.0 19.7 %fusion.62 = f32[2,2048,1536]{2,1,0:T(8,128)} fusion(bf16[2,2048,256]{2,1,0:T(8,128)(2,1)} %get-tuple-element.90, bf16[2,1536,256]{2,1,0:T(8,128)(2,1)} %param.24), kind=kOutput, calls=%fused_computation.122 | convolution fusion | flops 3221225472 | bytes 28835840 | tf_op jit(solution)/shard_map/erf,edf->erd/dot_general | solution.py:246
  404.7 21.5 %convolution_add_fusion = f32[2,2048,1536]{2,1,0:T(8,128)} fusion(f32[2,2048,1536]{2,1,0:T(8,128)} %fusion.62, bf16[2,2048,256]{2,1,0:T(8,128)(2,1)} %get-tuple-element.91, bf16[2,1536,256]{2,1,0:T(8,128)(2,1)} %param.25), kind=kOutput, calls=%fused_computation.4 | convolution fusion | flops 3227516928 | bytes 54001664 | tf_op jit(solution)/shard_map/erf,edf->erd/dot_general | solution.py:248
  426.3 12.8 copy.74
  439.1 5.8 all-to-all-start.1
  444.8 18.2 %reduce-scatter.5.cloned.1.call-done = f32[2,1024,1536]{2,1,0:T(8,128)} async-done(((f32[2,2048,1536]{2,1,0:T(8,128)}), f32[2,1024,1536]{2,1,0:T(8,128)}) %reduce-scatter.5.cloned.1.call-update) | async-done | bytes 12582928 | tf_op jit(solution)/shard_map/reduce_scatter | solution.py:249
  463.0 8.0 convert_element_type.120
  471.0 12.7 copy.78
  483.8 99.7 %all-to-all-done.1 = bf16[2,1024,1536]{2,0,1:T(2,128)(2,1)} async-done(((bf16[2,1024,1536]{2,0,1:T(2,128)(2,1)}), bf16[2,1024,1536]{2,0,1:T(2,128)(2,1)}, u32[]{:S(2)}, u32[]{:S(2)}) %all-to-all-start.1) | async-done | bytes 6291488 | tf_op jit(solution)/shard_map/all_to_all | solution.py:213
  583.5 4.7 all-to-all-start.3
  588.7 6.7 copy.75
  595.5 10.9 gather_fusion
  606.3 119.7 %all-to-all-done.3 = bf16[2,1024,1536]{2,0,1:T(2,128)(2,1)} async-done(((bf16[2,1024,1536]{2,0,1:T(2,128)(2,1)}), bf16[2,1024,1536]{2,0,1:T(2,128)(2,1)}, u32[]{:S(2)}, u32[]{:S(2)}) %all-to-all-start.3) | async-done | bytes 6291488 | tf_op jit(solution)/shard_map/all_to_all | solution.py:250
  726.0 6.7 copy.79
  732.7 10.9 gather_fusion.1
  743.5 8.7 fusion
  753.3 8.0 all-gather.11.cloned.1.call-done
  761.3 2.9 multiply_reduce_fusion
  764.7 9.8 all-gather.7.cloned.1.call-done
  774.5 2.8 subtract_add_fusion
  783.0 2.9 fusion.23
  788.7 3.0 fusion.27
  795.3 3.1 fusion.52
  798.5 10.5 fusion.66
  813.2 11.9 fusion.64
  825.1 12.0 fusion.65
  837.1 363.3 %all-reduce.13.cloned.1.call-done = (f32[1536,768]{1,0:T(8,128)}, f32[1536,256]{1,0:T(8,128)}, f32[1536,256]{1,0:T(8,128)}, f32[768,1536]{1,0:T(8,128)}) async-done(((f32[1536,768]{1,0:T(8,128)}, f32[1536,256]{1,0:T(8,128)}, f32[1536,256]{1,0:T(8,128)}, f32[768,1536]{1,0:T(8,128)}), (f32[1536,768]{1,0:T(8,128)}, f32[1536,256]{1,0:T(8,128)}, f32[1536,256]{1,0:T(8,128)}, ...) | async-done | bytes 12582928 | tf_op jit(solution)/shard_map/psum | solution.py:325
  1203.5 18.7 %all-reduce.11.cloned.1.call-done = f32[256,1536]{1,0:T(8,128)} async-done(((f32[256,1536]{1,0:T(8,128)}), f32[256,1536]{1,0:T(8,128)}) %all-reduce.11.cloned.1.call-update) | async-done | bytes 1572880 | tf_op jit(solution)/shard_map/psum | solution.py:320
  1222.1 2.9 fusion.21
  1225.1 37.3 %all-reduce = (f32[1536]{0:T(1024)S(1)}, f32[1536]{0:T(1024)S(1)}) all-reduce(f32[1536]{0:T(1024)S(1)} %get-tuple-element.56, f32[1536]{0:T(1024)S(1)} %copy-done.49), channel_id=1, replica_groups=mesh['dp'=2,'expert'=8,'tensor'=2] {'expert'}, use_global_device_ids=true, to_apply=%region_18.19 | all-reduce | flops 3072 | bytes 24576 | tf_op jit(solution)/shard_map/psum | solution.py:325
  1262.4 8.9 all-reduce.2
  1271.4 2.7 dynamic-slice_add_fusion
  1274.1 450.1 %all-reduce.15.cloned.1.call-done = (f32[1536,768]{1,0:T(8,128)}, f32[1536,256]{1,0:T(8,128)}, f32[1536,256]{1,0:T(8,128)}, f32[768,1536]{1,0:T(8,128)}, f32[2,1...) async-done(((f32[1536,768]{1,0:T(8,128)}, f32[1536,256]{1,0:T(8,128)}, f32[1536,256]{1,0:T(8,128)}, f32[768,1536]{1,0:T(8,128)}, ...) | async-done | bytes 22020112 | tf_op jit(solution)/shard_map/psum | solution.py:324
  1724.2 5.0 copy.123
  1732.7 2.4 copy.126
  (206 shorter events, 55.1 us)
Async XLA Ops:
  7.2 38.7 %copy-start = (bf16[768,1536]{1,0:T(8,128)(2,1)S(1)}, bf16[768,1536]{1,0:T(8,128)(2,1)}, u32[]{:S(2)}) copy-start(bf16[768,1536]{1,0:T(8,128)(2,1)} %param.23) | copy-start | bytes 7077892
  10.0 5.0 copy-start.34
  16.1 9.7 copy-start.6
  25.8 7.5 copy-start.37
  25.8 12.4 copy-start.38
  25.8 145.6 %all-to-all-start.2 = ((bf16[16,128,1536]{2,1,0:T(8,128)(2,1)}), bf16[16,128,1536]{2,1,0:T(8,128)(2,1)}, u32[]{:S(2)}, u32[]{:S(2)}) async-start(bf16[16,128,1536]{2,1,0:T(8,128)(2,1)} %bitcast.164), calls=%async_computation.3 | async-start | bytes 12582912 | tf_op jit(solution)/shard_map/all_to_all | solution.py:229
  33.2 144.3 %all-reduce.9.cloned.1.call-start = ((), (), s32[]{:S(2)}) async-start(), calls=%async_computation.6 | async-start | bytes 3145728 | tf_op jit(solution)/shard_map/psum | solution.py:188
  33.3 6.7 copy-start.14
  37.1 6.3 copy-start.47
  37.3 3.9 copy-start.23
  37.3 3.9 copy-start.25
  38.2 6.8 copy-start.44
  47.8 289.3 %all-gather.9.cloned.1.call-start = ((), (), s32[]{:S(2)}) async-start(), calls=%async_computation.10 | async-start | bytes 18874368 | tf_op jit(solution)/shard_map/all_gather | solution.py:230
  177.4 2.9 copy-start.46
  177.5 183.1 %all-gather.5.cloned.1.call-start = ((), (), s32[]{:S(2)}) async-start(), calls=%async_computation.7 | async-start | bytes 18874368 | tf_op jit(solution)/shard_map/all_gather | solution.py:203
  179.9 11.6 copy-start.52
  337.0 89.2 %reduce-scatter.3.cloned.1.call-start = ((), (), s32[]{:S(2)}) async-start(), calls=%async_computation.8 | async-start | bytes 18874368 | tf_op jit(solution)/shard_map/reduce_scatter | solution.py:210
  360.6 7.0 copy-start.16
  360.6 7.0 copy-start.58
  367.6 10.8 copy-start.20
  384.8 78.2 %reduce-scatter.5.cloned.1.call-start = ((), (), s32[]{:S(2)}) async-start(), calls=%async_computation.11 | async-start | bytes 37748736 | tf_op jit(solution)/shard_map/reduce_scatter | solution.py:249
  439.1 144.5 %all-to-all-start.1 = ((bf16[2,1024,1536]{2,0,1:T(2,128)(2,1)}), bf16[2,1024,1536]{2,0,1:T(2,128)(2,1)}, u32[]{:S(2)}, u32[]{:S(2)}) async-start(bf16[2,1024,1536]{2,0,1:T(2,128)(2,1)} %copy.74), calls=%async_computation.2 | async-start | bytes 12582912 | tf_op jit(solution)/shard_map/all_to_all | solution.py:213
  583.5 142.5 %all-to-all-start.3 = ((bf16[2,1024,1536]{2,0,1:T(2,128)(2,1)}), bf16[2,1024,1536]{2,0,1:T(2,128)(2,1)}, u32[]{:S(2)}, u32[]{:S(2)}) async-start(bf16[2,1024,1536]{2,0,1:T(2,128)(2,1)} %copy.78), calls=%async_computation.5 | async-start | bytes 12582912 | tf_op jit(solution)/shard_map/all_to_all | solution.py:250
  588.3 173.0 %all-gather.11.cloned.1.call-start = ((), (), s32[]{:S(2)}) async-start(), calls=%async_computation.12 | async-start | bytes 2359296 | tf_op jit(solution)/shard_map/all_gather | solution.py:259
  743.5 17.8 %copy-start.53 = (f32[256]{0:T(256)S(1)}, f32[256]{0:T(256)}, u32[]{:S(2)}) copy-start(f32[256]{0:T(256)} %copy-done.52) | copy-start | bytes 3076
  752.3 22.2 %copy-start.54 = (f32[256]{0:T(256)S(1)}, f32[256]{0:T(256)}, u32[]{:S(2)}) copy-start(f32[256]{0:T(256)} %get-tuple-element.102) | copy-start | bytes 3076
  752.3 22.2 %all-gather.7.cloned.1.call-start = ((), (), s32[]{:S(2)}) async-start(), calls=%async_computation.9 | async-start | bytes 2359296 | tf_op jit(solution)/shard_map/all_gather | solution.py:258
  753.0 447.4 %all-reduce.13.cloned.1.call-start = ((), (), s32[]{:S(2)}) async-start(), calls=%async_computation.14 | async-start | bytes 25165824 | tf_op jit(solution)/shard_map/psum | solution.py:325
  778.4 4.7 copy-start.51
  783.0 3.0 copy-start.9
  783.0 3.0 copy-start.19
  783.0 3.0 copy-start.45
  783.0 3.0 copy-start.57
  786.1 5.8 copy-start.35
  788.7 3.0 copy-start.24
  788.7 3.0 copy-start.26
  788.7 3.2 copy-start.39
  788.7 3.2 copy-start.48
  798.4 423.7 %all-reduce.11.cloned.1.call-start = ((), (), s32[]{:S(2)}) async-start(), calls=%async_computation.13 | async-start | bytes 3145728 | tf_op jit(solution)/shard_map/psum | solution.py:320
  798.5 10.5 copy-start.15
  812.9 911.3 %all-reduce.15.cloned.1.call-start = ((), (), s32[]{:S(2)}) async-start(), calls=%async_computation.15 | async-start | bytes 44040192 | tf_op jit(solution)/shard_map/psum | solution.py:324
  1203.4 21.7 %copy-start.49 = (f32[1536]{0:T(1024)S(1)}, f32[1536]{0:T(1024)}, u32[]{:S(2)}) copy-start(f32[1536]{0:T(1024)} %get-tuple-element.54) | copy-start | bytes 18436
  1724.2 5.0 copy-start.18
  1724.2 6.1 copy-start.17
  1729.2 3.5 copy-start.7
  1732.7 3.6 copy-start.12
  1736.3 3.0 copy-start.11
  1739.3 3.0 copy-start.10
  (24 other events, 33.6 us)
Sparse Core Ops, SparseCore 0:
  47.9 21.7 all-reduce.8
  177.6 23.4 all-gather.8
  337.1 23.4 all-gather.4
  384.9 22.6 reduce-scatter.2
  426.4 36.6 reduce-scatter.4
  752.4 8.8 all-gather.10
  763.5 10.9 all-gather.6
  798.6 401.7 all-reduce.12
  1202.8 19.3 all-reduce.10
  1225.9 498.2 all-reduce.14
